TPU v7x, 32 devices: a whole 2x2x4 slice. The times are simulated.
32 devices in a mesh: cone: 4 (over y, x), con: 8 (over z, core).
Axes of the slice: x: 2, y: 2, z: 4, core: 2. Of those that a mesh axis runs over, the one named last changes fastest.
Arguments:
- vectors: bfloat16 [4, 8192, 1024], P('cone', 'con'), may hold values from -0.1875 to 0.1875
- primal: bfloat16 [4, 1024, 1024], P('cone'), may hold values from -8 to 8, as said below
- dual_inverse: bfloat16 [4, 1024, 1024], P('cone'), may hold values from -8 to 8, as said below
- touches: int32 [4, 8], P('cone'), may hold values from 0 to 1, as said below
Outputs:
- slab: float32 [2048, 8192], P('cone', 'con')
Inputs may be any that keep to these rules, and one draw needn't show every extreme that they name: `primal`: symmetric and positive definite in every cone. `dual_inverse`: symmetric and positive definite in every cone. Every constraint block touches at least one cone.
All inputs are finite; a program needn't handle non-finite values.
Results may differ from a plain program's by a relative error of at most 0.00079.
Values may be sent and summed in bfloat16 or wider, within the bound.
No kernel may reach another device: no remote copies, remote signals or barrier semaphores. Data moves between devices by JAX's collectives and lax.ppermute only.
A program may use at most 128 MiB of HBM per device.

v0:
```python
import jax
import jax.numpy as jnp
from jax import lax
from jax.sharding import PartitionSpec as P

PANEL = 512


def broadcast(value, axis, source):
    kept = jnp.where(lax.axis_index(axis) == source, value, 0).astype(value.dtype)
    return lax.psum(kept, axis)


def shards(vectors, primal, dual_inverse, touches):
    con_count = lax.axis_size("con")
    cone_count = lax.axis_size("cone")
    con_place = lax.axis_index("con")
    cone_place = lax.axis_index("cone")
    per_block = vectors.shape[1]
    row_dev = PANEL * cone_count // con_count
    owners = con_count // cone_count
    touched = touches[0]
    own_flag = lax.dynamic_index_in_dim(touched, con_place, 0, keepdims=False)
    own_vectors = vectors[0] * own_flag.astype(jnp.bfloat16)
    primal_block = primal[0]
    dual_block = dual_inverse[0]
    row_vectors = lax.all_gather(own_vectors[:row_dev], "con", axis=0, tiled=True)
    row_primal = jnp.dot(row_vectors, primal_block, preferred_element_type=jnp.float32).astype(
        jnp.bfloat16
    )
    row_dual = jnp.dot(row_vectors, dual_block, preferred_element_type=jnp.float32).astype(
        jnp.bfloat16
    )
    contract = (((1,), (1,)), ((), ()))
    gram_primal = lax.dot_general(
        row_primal, own_vectors, contract, preferred_element_type=jnp.float32
    )
    gram_dual = lax.dot_general(row_dual, own_vectors, contract, preferred_element_type=jnp.float32)
    schur_slab = lax.psum_scatter(gram_primal * gram_dual, "cone", scatter_dimension=0, tiled=True)
    panel_block = broadcast(schur_slab, "cone", 0)
    leading_columns = panel_block[:, :row_dev]
    gathered = lax.all_gather(leading_columns, "con", axis=1, tiled=True)
    pivot_source = gathered[:, :PANEL]
    block_source = lax.dynamic_slice_in_dim(gathered, cone_place * PANEL, PANEL, 1)
    pivot_matrix = (pivot_source + pivot_source.T) * 0.5
    lower_factor = jnp.linalg.cholesky(pivot_matrix)
    combined = jnp.concatenate([panel_block, block_source], axis=1)
    solved = jax.scipy.linalg.solve_triangular(lower_factor, combined, lower=True)
    factor_rows = solved[:, :per_block]
    row_factor = solved[:, per_block:]
    updated = schur_slab - jnp.einsum(
        "kr,kc->rc", row_factor, factor_rows, precision=lax.Precision.HIGHEST
    )
    local_columns = jnp.arange(per_block, dtype=jnp.int32)
    pivot_column = (con_place < owners) & (local_columns < row_dev)
    remaining = jnp.where(pivot_column[None, :], 0.0, updated)
    return jnp.where(cone_place == 0, factor_rows, remaining)


def solution(mesh):
    in_specs = (
        P("cone", "con", None),
        P("cone", None, None),
        P("cone", None, None),
        P("cone", None),
    )
    out_specs = P("cone", "con")
    return jax.shard_map(shards, mesh=mesh, in_specs=in_specs, out_specs=out_specs, check_vma=False)
```

profile of v0, /device:TPU:0, one launch (start us, length us, event | category | flops | bytes accessed | tf_op | source)
XLA Modules:
  0.0 488.2 jit_solution(6037763311798876884)
XLA Ops:
  6.5 1.4 fusion.61
  7.9 2.4 broadcast_multiply_fusion
  10.3 1.3 copy-done.7
  12.5 49.7 %all-gather.6.cloned.1.call-done = bf16[1,2048,1024]{2,1,0:T(8,128)(2,1)} async-done(((bf16[1,256,1024]{2,1,0:T(8,128)(2,1)}), bf16[1,2048,1024]{2,1,0:T(8,128)(2,1)}) %all-gather.6.cloned.1.call-update) | async-done | bytes 4194320 | tf_op jit(solution)/shard_map/all_gather | solution.py:27
  62.2 7.1 %fusion.2 = bf16[2048,1024]{1,0:T(8,128)(2,1)S(1)} fusion(bf16[1,2048,1024]{2,1,0:T(8,128)(2,1)} %all-gather.6.cloned.1.call-done, bf16[1,1024,1024]{2,1,0:T(8,128)(2,1)S(1)} %copy-done), kind=kOutput, calls=%fused_computation.8 | convolution fusion | flops 4294967296 | bytes 10485760 | tf_op jit(solution)/shard_map/dot_general | solution.py:28
  69.3 4.6 fusion.5
  73.9 4.7 fusion
  78.7 6.8 %convolution_multiply_fusion = f32[2048,1024]{0,1:T(8,128)} fusion(f32[2048,1024]{0,1:T(8,128)S(1)} %fusion.5, bf16[2048,1024]{1,0:T(8,128)(2,1)S(1)} %fusion, bf16[1,1024,1024]{2,1,0:T(8,128)(2,1)S(1)} %copy-done.8), kind=kOutput, calls=%fused_computation.5 | convolution fusion | flops 4297064448 | bytes 23068672 | tf_op jit(solution)/shard_map/dot_general | solution.py:38
  85.5 85.2 %reduce-scatter.2.cloned.1.call-done = f32[512,1024]{0,1:T(8,128)} async-done(((f32[2048,1024]{0,1:T(8,128)}), f32[512,1024]{0,1:T(8,128)}) %reduce-scatter.2.cloned.1.call-update) | async-done | bytes 2097168 | tf_op jit(solution)/shard_map/reduce_scatter | solution.py:39
  170.7 3.1 broadcast_select_fusion
  174.1 69.2 %all-reduce.3.cloned.1.call-done = f32[512,1024]{0,1:T(8,128)} async-done(((f32[512,1024]{0,1:T(8,128)}), f32[512,1024]{0,1:T(8,128)}) %all-reduce.3.cloned.1.call-update) | async-done | bytes 2097168 | tf_op jit(solution)/shard_map/psum | solution.py:11
  243.3 1.9 slice.150
  245.3 47.0 %all-gather.4.cloned.1.call-done = f32[512,2048]{0,1:T(8,128)} async-done(((f32[512,256]{0,1:T(8,128)}), f32[512,2048]{0,1:T(8,128)}) %all-gather.4.cloned.1.call-update) | async-done | bytes 4194320 | tf_op jit(solution)/shard_map/all_gather | solution.py:42
  292.3 1.7 fusion.60
  294.3 1.4 fusion.31
  296.4 1.0 copy-done.9
  297.4 11.7 %cholesky.104 = f32[128,128]{1,0:T(8,128)S(1)} custom-call(f32[128,128]{1,0:T(8,128)S(1)} %cholesky.266), custom_call_target="Cholesky" | custom-call | tf_op jit(solution)/shard_map/jit(cholesky)/cholesky | solution.py:46
  309.1 1.1 cholesky.224
  310.2 9.8 %custom-call.31 = f32[1,128,128]{1,2,0:T(8,128)S(1)} custom-call(f32[1,128,128]{2,1,0:T(8,128)S(1)} %get-tuple-element.34), custom_call_target="InvertDiagBlocksLowerTriangular" | custom-call | tf_op jit(solution)/shard_map/jit(cholesky)/cholesky | solution.py:46
  320.0 1.9 constant_dynamic-update-slice_fusion.3
  321.9 1.2 convolution_subtract_fusion.3
  323.2 11.7 %cholesky.217 = f32[128,128]{1,0:T(8,128)S(1)} custom-call(f32[128,128]{1,0:T(8,128)S(1)} %cholesky.270), custom_call_target="Cholesky" | custom-call | tf_op jit(solution)/shard_map/jit(cholesky)/cholesky | solution.py:46
  335.6 10.2 %custom-call.32 = f32[1,128,128]{1,2,0:T(8,128)S(1)} custom-call(f32[1,128,128]{2,1,0:T(8,128)S(1)} %get-tuple-element.31), custom_call_target="InvertDiagBlocksLowerTriangular" | custom-call | tf_op jit(solution)/shard_map/jit(cholesky)/cholesky | solution.py:46
  345.8 0.9 convolution_dynamic-update-slice_fusion
  346.7 1.6 convolution_subtract_fusion.4
  348.3 11.7 %cholesky.238 = f32[128,128]{1,0:T(8,128)S(1)} custom-call(f32[128,128]{1,0:T(8,128)S(1)} %cholesky.275), custom_call_target="Cholesky" | custom-call | tf_op jit(solution)/shard_map/jit(cholesky)/cholesky | solution.py:46
  361.3 9.8 %custom-call.33 = f32[1,128,128]{1,2,0:T(8,128)S(1)} custom-call(f32[1,128,128]{2,1,0:T(8,128)S(1)} %get-tuple-element.28), custom_call_target="InvertDiagBlocksLowerTriangular" | custom-call | tf_op jit(solution)/shard_map/jit(cholesky)/cholesky | solution.py:46
  372.0 1.4 convolution_subtract_fusion.5
  373.4 11.9 %cholesky.255 = f32[128,128]{1,0:T(8,128)S(1)} custom-call(f32[128,128]{1,0:T(8,128)S(1)} %convolution_subtract_fusion.5), custom_call_target="Cholesky" | custom-call | tf_op jit(solution)/shard_map/jit(cholesky)/cholesky | solution.py:46
  389.8 2.3 select_select_fusion.1
  392.1 14.0 %while.1 = (s32[]{:T(128)}, f32[512,512]{1,0:T(8,128)}, s32[4,2]{0,1:T(2,128)S(1)}, f32[4,128,128]{2,1,0:T(8,128)}, s32[]{:T(128)}) while((s32[]{:T(128)}, f32[512,512]{1,0:T(8,128)}, s32[4,2]{0,1:T(2,128)S(1)}, f32[4,128,128]{2,1,0:T(8,128)}, s32[]{:T(128)}) %tuple.28), condition=%wide.while_cond, body=%wide.while_body.sunk | while | flops 2 | bytes 132705 | solution.py:48
  392.7 2.9 bitcast_dynamic-update-slice_fusion.2
  396.3 2.9 bitcast_dynamic-update-slice_fusion.2
  399.8 2.9 bitcast_dynamic-update-slice_fusion.2
  403.3 2.8 bitcast_dynamic-update-slice_fusion.2
  406.1 40.1 %custom-call.34 = f32[4,128,128]{1,2,0:T(8,128)S(1)} custom-call(f32[4,128,128]{2,1,0:T(8,128)} %get-tuple-element.12), custom_call_target="InvertDiagBlocksLowerTriangular" | custom-call | tf_op jit(solution)/shard_map/jit(_solve_triangular)/triangular_solve | solution.py:48
  446.3 1.8 fusion.34
  448.0 2.3 copy.9
  450.3 2.6 convolution_subtract_fusion.2
  452.9 1.7 fusion.48
  454.7 2.3 copy.10
  456.9 4.1 convolution_subtract_fusion
  461.0 1.8 fusion.46
  462.8 2.3 copy.11
  465.1 6.1 %convolution_subtract_fusion.1 = f32[128,1536]{0,1:T(8,128)S(1)} fusion(f32[128,1536]{1,0:T(8,128)} %fusion.46, f32[128,1536]{1,0:T(8,128)} %fusion.48, f32[128,1536]{1,0:T(8,128)} %fusion.34, f32[512,512]{0,1:T(8,128)S(1)} %get-tuple-element.24, f32[512,1024]{0,1:T(8,128)S(1)} %copy-done.2, f32[512,512]{1,0:T(8,128)} %get-tuple-element.93), kind=kOutput, calls=%fused_computation.18 | convolution fusion | flops 907542528 | bytes 6488064 | tf_op jit(solution)/shard_map/jit(_solve_triangular)/triangular_solve | solution.py:48
  472.2 1.4 copy-done.3
  473.6 5.0 %select_select_fusion = f32[512,1024]{0,1:T(8,128)} fusion(f32[512,1024]{0,1:T(8,128)S(1)} %copy-done.3, f32[512,1536]{0,1:T(8,128)S(1)} %pad_maximum_fusion, f32[128,1536]{0,1:T(8,128)S(1)} %fusion.45, f32[128,1536]{0,1:T(8,128)S(1)} %copy-done.6, f32[128,1536]{0,1:T(8,128)S(1)} %copy-done.5, f32[128,1536]{0,1:T(8,128)S(1)} %copy-done.4, ...), kind=kOutput, calls=%fused_computation.29 | convolution fusion | flops 3223584768 | bytes 11535361 | tf_op jit(solution)/shard_map/kr,kc->rc/dot_general | solution.py:51
  478.6 2.9 copy.14
  (58 shorter events, 10.6 us)
Async XLA Ops:
  6.5 55.7 %copy-start = (bf16[1,1024,1024]{2,1,0:T(8,128)(2,1)S(1)}, bf16[1,1024,1024]{2,1,0:T(8,128)(2,1)}, u32[]{:S(2)}) copy-start(bf16[1,1024,1024]{2,1,0:T(8,128)(2,1)} %param.5) | copy-start | bytes 6291460
  6.5 55.7 %all-gather.6.cloned.1.call-start = ((), (), s32[]{:S(2)}) async-start(), calls=%async_computation.4 | async-start | bytes 4718592 | tf_op jit(solution)/shard_map/all_gather | solution.py:27
  10.3 1.3 copy-start.7
  12.5 158.2 %reduce-scatter.2.cloned.1.call-start = ((), (), s32[]{:S(2)}) async-start(), calls=%async_computation.1 | async-start | bytes 10485760 | tf_op jit(solution)/shard_map/reduce_scatter | solution.py:39
  62.2 7.1 %copy-start.8 = (bf16[1,1024,1024]{2,1,0:T(8,128)(2,1)S(1)}, bf16[1,1024,1024]{2,1,0:T(8,128)(2,1)}, u32[]{:S(2)}) copy-start(bf16[1,1024,1024]{2,1,0:T(8,128)(2,1)} %copy-done.7) | copy-start | bytes 6291460
  69.3 4.6 copy-start.10
  69.3 4.6 copy-start.11
  85.5 157.9 %all-reduce.3.cloned.1.call-start = ((), (), s32[]{:S(2)}) async-start(), calls=%async_computation.2 | async-start | bytes 4194304 | tf_op jit(solution)/shard_map/psum | solution.py:11
  173.9 118.4 %all-gather.4.cloned.1.call-start = ((), (), s32[]{:S(2)}) async-start(), calls=%async_computation.3 | async-start | bytes 4718592 | tf_op jit(solution)/shard_map/all_gather | solution.py:42
  296.4 1.0 copy-start.9
  346.7 99.6 %copy-start.2 = (f32[512,1024]{0,1:T(8,128)S(1)}, f32[512,1024]{0,1:T(8,128)}, u32[]{:S(2)}) copy-start(f32[512,1024]{0,1:T(8,128)} %all-reduce.3.cloned.1.call-done) | copy-start | bytes 6291460
  465.1 6.9 %copy-start.4 = (f32[128,1536]{0,1:T(8,128)S(1)}, f32[128,1536]{0,1:T(8,128)}, u32[]{:S(2)}) copy-start(f32[128,1536]{0,1:T(8,128)} %copy.9) | copy-start | bytes 2359300
  465.1 6.9 %copy-start.5 = (f32[128,1536]{0,1:T(8,128)S(1)}, f32[128,1536]{0,1:T(8,128)}, u32[]{:S(2)}) copy-start(f32[128,1536]{0,1:T(8,128)} %copy.10) | copy-start | bytes 2359300
  465.1 6.9 %copy-start.6 = (f32[128,1536]{0,1:T(8,128)S(1)}, f32[128,1536]{0,1:T(8,128)}, u32[]{:S(2)}) copy-start(f32[128,1536]{0,1:T(8,128)} %copy.11) | copy-start | bytes 2359300
  472.0 1.6 copy-start.3
  473.6 7.9 %copy-start.1 = (bf16[1,1024,1024]{2,1,0:T(8,128)(2,1)S(1)}, bf16[1,1024,1024]{2,1,0:T(8,128)(2,1)}, u32[]{:S(2)}) copy-start(bf16[1,1024,1024]{2,1,0:T(8,128)(2,1)} %param.5) | copy-start | bytes 6291460
Sparse Core Ops, SparseCore 0:
  12.6 49.5 all-gather.5
  85.6 85.1 reduce-scatter.1
  174.0 69.2 all-reduce.2
  245.4 46.8 all-gather.3
where the time goes:
time: 497 us; the launch traced here: 488 us
  waiting for transfers between devices  251 us (51%)
  other arithmetic  132 us (27%)
  matrix products  54.8 us (11%)
  local copies, waits for them, and re-layouts  33.7 us (7%)
  between operations  16.2 us (3%)
    reduce_scatter x1, waiting for transfers between devices, shards(): lax.psum_scatter(gram_primal * gram_dual, 'cone', scatter_dimension=0, ti...  85.2 us
    another operation x14, other arithmetic, shards(): lower_factor = jnp.linalg.cholesky(pivot_matrix)  80.8 us
    psum x1, waiting for transfers between devices, broadcast(): return lax.psum(kept, axis)  69.2 us
    all_gather x1, waiting for transfers between devices, shards(): lax.all_gather(own_vectors[:row_dev], 'con', axis=0, tiled=True)  49.7 us
    all_gather x1, waiting for transfers between devices, shards(): gathered = lax.all_gather(leading_columns, 'con', axis=1, tiled=True)  47 us
    another operation x4, other arithmetic, shards(): jax.scipy.linalg.solve_triangular(lower_factor, combined, lower=True)  42.7 us
    another operation x7, matrix products, shards(): jax.scipy.linalg.solve_triangular(lower_factor, combined, lower=True)  18.8 us
    another operation x12, local copies, waits for them, and re-layouts  14 us
  transfers between devices with their start and end apart: 4, of which 4 were waited for; matrix products, arithmetic and copies ran while one was open for 0% of the time, Pallas kernels for 0%

commit v1 on v0

--- a/solution.py
+++ b/solution.py
@@ -4,6 +4,27 @@
 from jax.sharding import PartitionSpec as P
 
 PANEL = 512
+
+
+def in_order(parts, dim):
+    parts = jnp.moveaxis(parts, 0, dim)
+    dims = parts.shape
+    return parts.reshape(*dims[:dim], dims[dim] * dims[dim + 1], *dims[dim + 2 :])
+
+
+def grow_blocks(x, axis):
+    size, index = (lax.axis_size(axis), lax.axis_index(axis))
+    tiles, bit = (x[None], 1)
+    while bit < size:
+        other = lax.ppermute(tiles, axis, [(i, i ^ bit) for i in range(size)])
+        low = index & bit == 0
+        tiles = jnp.concatenate([jnp.where(low, tiles, other), jnp.where(low, other, tiles)])
+        bit *= 2
+    return tiles
+
+
+def collect(value, axis, dim):
+    return in_order(grow_blocks(value, axis), dim)
 
 
 def broadcast(value, axis, source):
@@ -39,7 +60,7 @@
     schur_slab = lax.psum_scatter(gram_primal * gram_dual, "cone", scatter_dimension=0, tiled=True)
     panel_block = broadcast(schur_slab, "cone", 0)
     leading_columns = panel_block[:, :row_dev]
-    gathered = lax.all_gather(leading_columns, "con", axis=1, tiled=True)
+    gathered = collect(leading_columns, "con", 1)
     pivot_source = gathered[:, :PANEL]
     block_source = lax.dynamic_slice_in_dim(gathered, cone_place * PANEL, PANEL, 1)
     pivot_matrix = (pivot_source + pivot_source.T) * 0.5

time: 497 us -> 564 us (1.13)
  waiting for transfers between devices: 251 us -> 321 us
  matrix products: 54.8 us -> 48.1 us
    ppermute x0 -> x3, waiting for transfers between devices: none -> 116 us  [grow_blocks(): other = lax.ppermute(tiles, axis, [(i, i ^ bit) for i in range(size)])]
    all_gather x1 -> x0, waiting for transfers between devices: 47 us -> none  [shards(): gathered = lax.all_gather(leading_columns, 'con', axis=1, tiled=True)]
    dot_general x2 -> x0, matrix products: 11.8 us -> none  [the longest x1 7.07 us: shards(): jnp.dot(row_vectors, primal_block, preferred_element_type=jnp.float32)]
    another operation x7, matrix products: 18.8 us -> 9.39 us  [shards(): jax.scipy.linalg.solve_triangular(lower_factor, combined, lower=True)]
    dot_general x1, matrix products: 4.55 us -> 13.2 us  [shards(): lax.dot_general(row_primal, own_vectors, contract, preferred_element_type...]
    dot_general x1, matrix products: 6.77 us -> 15 us  [shards(): lax.dot_general(row_dual, own_vectors, contract, preferred_element_type=j...]
    another operation x4 -> x1, local copies, waits for them, and re-layouts: 6.87 us -> 0.01 us  [shards(): jax.scipy.linalg.solve_triangular(lower_factor, combined, lower=True)]
    transpose x0 -> x1, local copies, waits for them, and re-layouts: none -> 5.8 us  [in_order(): parts = jnp.moveaxis(parts, 0, dim)]
  transfers between devices with their start and end apart: 4 -> 6, of which waited for: 4 -> 6; matrix products, arithmetic and copies ran while one was open for 0% -> 0% of each run, Pallas kernels for 0% -> 0%
where the time goes in v1:
time: 564 us; the launch traced here: 556 us
  waiting for transfers between devices  321 us (57%)
  other arithmetic  137 us (24%)
  matrix products  48.1 us (9%)
  local copies, waits for them, and re-layouts  30.1 us (5%)
  between operations  16 us (3%)
    ppermute x3, waiting for transfers between devices, grow_blocks(): other = lax.ppermute(tiles, axis, [(i, i ^ bit) for i in range(size)])  116 us
    reduce_scatter x1, waiting for transfers between devices, shards(): lax.psum_scatter(gram_primal * gram_dual, 'cone', scatter_dimension=0, ti...  85.2 us
    another operation x14, other arithmetic, shards(): lower_factor = jnp.linalg.cholesky(pivot_matrix)  78.7 us
    psum x1, waiting for transfers between devices, broadcast(): return lax.psum(kept, axis)  69.4 us
    all_gather x1, waiting for transfers between devices, shards(): lax.all_gather(own_vectors[:row_dev], 'con', axis=0, tiled=True)  49.7 us
    another operation x4, other arithmetic, shards(): jax.scipy.linalg.solve_triangular(lower_factor, combined, lower=True)  41.4 us
    dot_general x1, matrix products, shards(): lax.dot_general(row_dual, own_vectors, contract, preferred_element_type=j...  15 us
    another operation x12, local copies, waits for them, and re-layouts  13.7 us
  transfers between devices with their start and end apart: 6, of which 6 were waited for; matrix products, arithmetic and copies ran while one was open for 0% of the time, Pallas kernels for 0%

profile of v1, /device:TPU:0, one launch (start us, length us, event | category | flops | bytes accessed | tf_op | source)
XLA Modules:
  0.0 556.0 jit_solution(15795564956205927200)
XLA Ops:
  6.5 1.4 fusion.77
  7.9 2.4 broadcast_multiply_fusion
  10.3 1.3 copy-done.4
  12.5 49.7 %all-gather.3.cloned.1.call-done = bf16[1,2048,1024]{2,1,0:T(8,128)(2,1)} async-done(((bf16[1,256,1024]{2,1,0:T(8,128)(2,1)}), bf16[1,2048,1024]{2,1,0:T(8,128)(2,1)}) %all-gather.3.cloned.1.call-update) | async-done | bytes 4194320 | tf_op jit(solution)/shard_map/all_gather | solution.py:48
  62.2 13.2 %fusion.5 = f32[2048,1024]{1,0:T(8,128)} fusion(bf16[1,1024,1024]{2,1,0:T(8,128)(2,1)} %copy-done.4, bf16[1,2048,1024]{2,1,0:T(8,128)(2,1)} %all-gather.3.cloned.1.call-done, bf16[1,1024,1024]{2,1,0:T(8,128)(2,1)S(1)} %copy-done), kind=kOutput, calls=%fused_computation.12 | convolution fusion | flops 8592031744 | bytes 16777216 | tf_op jit(solution)/shard_map/dot_general | solution.py:56
  75.4 15.0 %convolution_multiply_fusion = f32[2048,1024]{1,0:T(8,128)} fusion(f32[2048,1024]{1,0:T(8,128)} %fusion.5, bf16[1,1024,1024]{2,1,0:T(8,128)(2,1)} %copy-done.4, bf16[1,2048,1024]{2,1,0:T(8,128)(2,1)} %all-gather.3.cloned.1.call-done, bf16[1,1024,1024]{2,1,0:T(8,128)(2,1)} %param.6), kind=kOutput, calls=%fused_computation.5 | convolution fusion | flops 8594128896 | bytes 25165824 | tf_op jit(solution)/shard_map/dot_general | solution.py:59
  90.5 85.2 %reduce-scatter.2.cloned.1.call-done = f32[512,1024]{1,0:T(8,128)} async-done(((f32[2048,1024]{1,0:T(8,128)}), f32[512,1024]{1,0:T(8,128)}) %reduce-scatter.2.cloned.1.call-update) | async-done | bytes 2097168 | tf_op jit(solution)/shard_map/reduce_scatter | solution.py:60
  175.7 3.2 broadcast_select_fusion
  178.9 69.4 %all-reduce.3.cloned.1.call-done = f32[512,1024]{1,0:T(8,128)} async-done(((f32[512,1024]{1,0:T(8,128)}), f32[512,1024]{1,0:T(8,128)}) %all-reduce.3.cloned.1.call-update) | async-done | bytes 2097168 | tf_op jit(solution)/shard_map/psum | solution.py:32
  248.3 1.1 slice_bitcast_fusion
  249.5 1.9 collective-permute-done
  251.4 1.1 broadcast_select_fusion.6
  252.6 1.6 collective-permute-start.1
  254.1 23.8 %collective-permute-done.1 = f32[2,512,256]{2,1,0:T(8,128)} collective-permute-done((f32[2,512,256]{2,1,0:T(8,128)S(1)}, f32[2,512,256]{2,1,0:T(8,128)}, u32[]{:S(2)}, u32[]{:S(2)}) %collective-permute-start.1) | collective-permute-done | bytes 1048608 | tf_op jit(solution)/shard_map/ppermute | solution.py:19
  278.0 1.4 broadcast_select_fusion.4
  279.4 1.5 pad_maximum_fusion.1
  280.9 2.4 collective-permute-start.2
  283.3 90.6 %collective-permute-done.2 = f32[4,512,256]{2,1,0:T(8,128)} collective-permute-done((f32[4,512,256]{2,1,0:T(8,128)}, f32[4,512,256]{2,1,0:T(8,128)}, u32[]{:S(2)}, u32[]{:S(2)}) %collective-permute-start.2) | collective-permute-done | bytes 2097184 | tf_op jit(solution)/shard_map/ppermute | solution.py:19
  373.9 1.9 broadcast_select_fusion.2
  375.8 2.2 maximum_bitcast_fusion
  378.0 5.8 %copy.5 = f32[512,8,256]{0,2,1:T(8,128)} copy(f32[512,8,256]{2,0,1:T(8,128)} %maximum_bitcast_fusion) | data formatting | bytes 8388608 | tf_op jit(solution)/shard_map/transpose | solution.py:10
  383.8 2.7 fusion.76
  386.8 1.4 fusion.47
  388.8 1.0 copy-done.5
  389.8 11.7 %cholesky.104 = f32[128,128]{1,0:T(8,128)S(1)} custom-call(f32[128,128]{1,0:T(8,128)S(1)} %cholesky.266), custom_call_target="Cholesky" | custom-call | tf_op jit(solution)/shard_map/jit(cholesky)/cholesky | solution.py:67
  401.7 9.8 %custom-call.31 = f32[1,128,128]{1,2,0:T(8,128)S(1)} custom-call(f32[1,128,128]{2,1,0:T(8,128)S(1)} %get-tuple-element.40), custom_call_target="InvertDiagBlocksLowerTriangular" | custom-call | tf_op jit(solution)/shard_map/jit(cholesky)/cholesky | solution.py:67
  411.5 1.2 constant_dynamic-update-slice_fusion.3
  412.8 1.3 convolution_subtract_fusion.3
  414.0 11.7 %cholesky.217 = f32[128,128]{1,0:T(8,128)S(1)} custom-call(f32[128,128]{1,0:T(8,128)S(1)} %cholesky.270), custom_call_target="Cholesky" | custom-call | tf_op jit(solution)/shard_map/jit(cholesky)/cholesky | solution.py:67
  425.8 10.0 %custom-call.32 = f32[1,128,128]{1,2,0:T(8,128)S(1)} custom-call(f32[1,128,128]{2,1,0:T(8,128)S(1)} %get-tuple-element.37), custom_call_target="InvertDiagBlocksLowerTriangular" | custom-call | tf_op jit(solution)/shard_map/jit(cholesky)/cholesky | solution.py:67
  436.0 1.3 convolution_subtract_fusion.4
  437.3 11.7 %cholesky.238 = f32[128,128]{1,0:T(8,128)S(1)} custom-call(f32[128,128]{1,0:T(8,128)S(1)} %cholesky.275), custom_call_target="Cholesky" | custom-call | tf_op jit(solution)/shard_map/jit(cholesky)/cholesky | solution.py:67
  449.7 9.8 %custom-call.33 = f32[1,128,128]{1,2,0:T(8,128)S(1)} custom-call(f32[1,128,128]{2,1,0:T(8,128)S(1)} %get-tuple-element.34), custom_call_target="InvertDiagBlocksLowerTriangular" | custom-call | tf_op jit(solution)/shard_map/jit(cholesky)/cholesky | solution.py:67
  459.7 1.2 convolution_subtract_fusion.5
  461.0 11.9 %cholesky.255 = f32[128,128]{1,0:T(8,128)S(1)} custom-call(f32[128,128]{1,0:T(8,128)S(1)} %convolution_subtract_fusion.5), custom_call_target="Cholesky" | custom-call | tf_op jit(solution)/shard_map/jit(cholesky)/cholesky | solution.py:67
  476.6 1.1 select_select_fusion.1
  477.8 13.7 %while.1 = (s32[]{:T(128)}, f32[512,512]{1,0:T(8,128)}, s32[4,2]{0,1:T(2,128)S(1)}, f32[4,128,128]{2,1,0:T(8,128)}, s32[]{:T(128)}) while((s32[]{:T(128)}, f32[512,512]{1,0:T(8,128)}, s32[4,2]{0,1:T(2,128)S(1)}, f32[4,128,128]{2,1,0:T(8,128)}, s32[]{:T(128)}) %tuple.31), condition=%wide.while_cond, body=%wide.while_body.sunk | while | flops 2 | bytes 132705 | solution.py:69
  478.4 2.8 bitcast_dynamic-update-slice_fusion.2
  481.8 2.8 bitcast_dynamic-update-slice_fusion.2
  485.3 2.8 bitcast_dynamic-update-slice_fusion.2
  488.7 2.8 bitcast_dynamic-update-slice_fusion.2
  491.5 40.1 %custom-call.34 = f32[4,128,128]{1,2,0:T(8,128)S(1)} custom-call(f32[4,128,128]{2,1,0:T(8,128)} %get-tuple-element.12), custom_call_target="InvertDiagBlocksLowerTriangular" | custom-call | tf_op jit(solution)/shard_map/jit(_solve_triangular)/triangular_solve | solution.py:69
  531.6 1.6 copy.8
  534.0 1.6 convolution_subtract_fusion.2
  536.5 1.9 convolution_subtract_fusion
  539.2 2.5 convolution_subtract_fusion.1
  542.8 1.4 copy-done.3
  544.2 5.1 select_select_fusion
  (51 shorter events, 10.8 us)
Async XLA Ops:
  6.5 55.7 %copy-start = (bf16[1,1024,1024]{2,1,0:T(8,128)(2,1)S(1)}, bf16[1,1024,1024]{2,1,0:T(8,128)(2,1)}, u32[]{:S(2)}) copy-start(bf16[1,1024,1024]{2,1,0:T(8,128)(2,1)} %param.5) | copy-start | bytes 6291460
  6.5 55.7 %all-gather.3.cloned.1.call-start = ((), (), s32[]{:S(2)}) async-start(), calls=%async_computation.3 | async-start | bytes 4718592 | tf_op jit(solution)/shard_map/all_gather | solution.py:48
  10.3 1.3 copy-start.4
  12.5 163.3 %reduce-scatter.2.cloned.1.call-start = ((), (), s32[]{:S(2)}) async-start(), calls=%async_computation.1 | async-start | bytes 10485760 | tf_op jit(solution)/shard_map/reduce_scatter | solution.py:60
  90.5 157.9 %all-reduce.3.cloned.1.call-start = ((), (), s32[]{:S(2)}) async-start(), calls=%async_computation.2 | async-start | bytes 4194304 | tf_op jit(solution)/shard_map/psum | solution.py:32
  249.4 2.0 collective-permute-start
  252.6 25.4 %collective-permute-start.1 = (f32[2,512,256]{2,1,0:T(8,128)S(1)}, f32[2,512,256]{2,1,0:T(8,128)}, u32[]{:S(2)}, u32[]{:S(2)}) collective-permute-start(f32[2,512,256]{2,1,0:T(8,128)S(1)} %pad_maximum_fusion.2), channel_id=1, source_target_pairs={{0,2},{1,3},{2,0},{3,1},{4,6},{5,7},{6,4},{7,5},{8,10},{9,11},{10,... | collective-permute-start | bytes 3145736 | tf_op jit(solution)/shard_map/ppermute | solution.py:19
  280.9 93.0 %collective-permute-start.2 = (f32[4,512,256]{2,1,0:T(8,128)}, f32[4,512,256]{2,1,0:T(8,128)}, u32[]{:S(2)}, u32[]{:S(2)}) collective-permute-start(f32[4,512,256]{2,1,0:T(8,128)} %pad_maximum_fusion.1), channel_id=1, source_target_pairs={{0,4},{1,5},{2,6},{3,7},{4,0},{5,1},{6,2},{7,3},{8,12},{9,13},{10,... | collective-permute-start | bytes 6291464 | tf_op jit(solution)/shard_map/ppermute | solution.py:19
  388.8 1.0 copy-start.5
  476.6 56.5 %copy-start.2 = (f32[512,1024]{1,0:T(8,128)S(1)}, f32[512,1024]{1,0:T(8,128)}, u32[]{:S(2)}) copy-start(f32[512,1024]{1,0:T(8,128)} %all-reduce.3.cloned.1.call-done) | copy-start | bytes 6291460
  542.6 1.6 copy-start.3
  544.2 5.1 copy-start.1
Sparse Core Ops, SparseCore 0:
  12.6 49.5 all-gather.2
  90.6 85.1 reduce-scatter.1
  179.1 69.2 all-reduce.2
